TPU v7x, 512 devices: a whole 4x8x8 slice. The times are simulated.
512 devices in a mesh: group: 16 (over z, core), member: 32 (over y, x).
Axes of the slice: x: 4, y: 8, z: 8, core: 2. Of those that a mesh axis runs over, the one named last changes fastest.
Arguments:
- tokens: bfloat16 [8192, 7168], P('group', 'member'), may hold values from -6 to 6
- grad_output: bfloat16 [8192, 7168], P('group', 'member'), may hold values from -6 to 6
- gate_prob: bfloat16 [8192, 16], P('group'), may hold values from 0.099609375 to 1
- w_gate: bfloat16 [16, 7168, 1024], P('group', 'member'), may hold values from -0.0625 to 0.0625
- w_up: bfloat16 [16, 7168, 1024], P('group', 'member'), may hold values from -0.0625 to 0.0625
- w_down: bfloat16 [16, 1024, 7168], P('group', None, 'member'), may hold values from -0.1875 to 0.1875
- expert_slot: int32 [16], replicated, may hold values from 0 to 15, each once
- block_counts: int32 [16, 16], replicated, may hold values from 0 to 10, as said below
- block_lists: int32 [16, 16, 10], P('group'), may hold values from 0 to 15, as said below
Outputs:
- layer_output: bfloat16 [8192, 7168], P('group', 'member')
- grad_input: bfloat16 [8192, 7168], P('group', 'member')
- grad_w_gate: bfloat16 [16, 7168, 1024], P('group', 'member')
- grad_w_up: bfloat16 [16, 7168, 1024], P('group', 'member')
- grad_w_down: bfloat16 [16, 1024, 7168], P('group', None, 'member')
Inputs may be any that keep to these rules, and one draw needn't show every extreme that they name: `block_counts`: each group sends blocks to 1 to 2 experts and some group to exactly 2; each expert receives blocks from 1 to 2 groups and some expert from exactly 2; some count equals 10. `block_lists`: the first block_counts[g, e] entries of a list are distinct blocks of group g; later entries are block numbers that play no part. `expert_slot`: a permutation of the slots; slot s lies on group s.
All inputs are finite; a program needn't handle non-finite values.
Results may differ from a plain program's by a relative error of at most 0.034.
Values may be sent and summed in bfloat16 or wider, within the bound.
No kernel may reach another device: no remote copies, remote signals or barrier semaphores. Data moves between devices by JAX's collectives and lax.ppermute only.
A program may use at most 64 MiB of HBM per device.

v0:
```python
import jax
import jax.numpy as jnp
from jax import lax
from jax.sharding import PartitionSpec as P

MAXE = 2
BLK = 32


def expert_pass(input_rows, rows_dy, rows_p, gate_w, up_w, down_w):
    form_in, form_out, form_back, form_dx = (
        "xjb,bxl->xjl",
        "wzq,wqi->wzi",
        "eph,ezh->epz",
        "bya,qba->byq",
    )
    part_gate = jnp.einsum(form_in, input_rows, gate_w, preferred_element_type=jnp.float32)
    part_up = jnp.einsum(form_in, input_rows, up_w, preferred_element_type=jnp.float32)
    gate, up = (
        lax.psum(part_gate.astype(jnp.bfloat16), "member").astype(jnp.float32),
        lax.psum(part_up.astype(jnp.bfloat16), "member").astype(jnp.float32),
    )
    sigma = jax.nn.sigmoid(gate)
    hidden_state = (gate * sigma * up).astype(jnp.bfloat16)
    outcome = (
        rows_p[:, :, None]
        * jnp.einsum(form_out, hidden_state, down_w, preferred_element_type=jnp.float32)
    ).astype(jnp.bfloat16)
    gradient_rows = (rows_p[:, :, None] * rows_dy.astype(jnp.float32)).astype(jnp.bfloat16)
    part_hidden = jnp.einsum(form_back, gradient_rows, down_w, preferred_element_type=jnp.float32)
    grad_hidden = lax.psum(part_hidden.astype(jnp.bfloat16), "member").astype(jnp.float32)
    gate_gradient = (grad_hidden * up * sigma * (1.0 + gate * (1.0 - sigma))).astype(jnp.bfloat16)
    up_gradient = (grad_hidden * gate * sigma).astype(jnp.bfloat16)
    rows_dx = (
        jnp.einsum(form_dx, gate_gradient, gate_w, preferred_element_type=jnp.float32)
        + jnp.einsum(form_dx, up_gradient, up_w, preferred_element_type=jnp.float32)
    ).astype(jnp.bfloat16)
    weight_gate = jnp.einsum(
        "tgw,tgs->wts", input_rows, gate_gradient, preferred_element_type=jnp.float32
    ).astype(jnp.bfloat16)
    weight_up = jnp.einsum(
        "tgw,tgs->wts", input_rows, up_gradient, preferred_element_type=jnp.float32
    ).astype(jnp.bfloat16)
    weight_down = jnp.einsum(
        "sui,sug->sig", hidden_state, gradient_rows, preferred_element_type=jnp.float32
    ).astype(jnp.bfloat16)
    return (outcome, rows_dx, weight_gate, weight_up, weight_down)


def gather_rows(blocked, listed, keep_rows):
    picked = jnp.take(blocked, listed, axis=0)
    return picked * keep_rows[:, :, None, None].astype(blocked.dtype)


def place_rows(pieces, listed, keep_rows, block_total):
    placing = (
        (listed[:, :, None] == jnp.arange(block_total, dtype=jnp.int32)[None, None, :])
        & (keep_rows[:, :, None] > 0)
    ).astype(jnp.bfloat16)
    return jnp.einsum("kbn,kbtd->ntd", placing, pieces, preferred_element_type=jnp.float32)


def body(
    tokens, grad_output, gate_prob, w_gate, w_up, w_down, expert_slot, block_counts, block_lists
):
    width_share = tokens.shape[1]
    hidden_total = w_gate.shape[2]
    group_total = lax.axis_size("group")
    piece_size = hidden_total // group_total
    block_total = tokens.shape[0] // BLK
    entry_total = block_lists.shape[2]
    row_total = entry_total * BLK
    experts_total = block_counts.shape[1]
    group_index = lax.axis_index("group")
    entry_ids = jnp.arange(entry_total, dtype=jnp.int32)
    group_ids = jnp.arange(group_total, dtype=jnp.int32)
    ranks_wanted = jnp.arange(MAXE, dtype=jnp.int32)
    tok_blocks = tokens.reshape(block_total, BLK, width_share)
    grad_blocks = grad_output.reshape(block_total, BLK, width_share)
    prob_blocks = gate_prob.reshape(block_total, BLK, experts_total)
    my_counts = lax.dynamic_index_in_dim(block_counts, group_index, 0, keepdims=False)
    my_lists = block_lists[0]
    in_use = (block_counts > 0).astype(jnp.int32)
    use_rank = jnp.cumsum(in_use, axis=1) - 1
    selected = in_use[:, None, :] * (use_rank[:, None, :] == ranks_wanted[None, :, None]).astype(
        jnp.int32
    )
    need_slot = jnp.sum(selected * expert_slot[None, None, :], axis=2)
    need_valid = jnp.sum(selected, axis=2)
    own_select = lax.dynamic_index_in_dim(selected, group_index, 0, keepdims=False)
    my_amount = jnp.sum(own_select * my_counts[None, :], axis=1)
    listed = jnp.sum(own_select[:, :, None] * my_lists[None, :, :], axis=1)
    keep_rows = (entry_ids[None, :] < my_amount[:, None]).astype(jnp.int32)
    input_rows = gather_rows(tok_blocks, listed, keep_rows).reshape(MAXE, row_total, width_share)
    rows_dy = gather_rows(grad_blocks, listed, keep_rows).reshape(MAXE, row_total, width_share)
    prob_rows = gather_rows(prob_blocks, listed, keep_rows)
    rows_p = jnp.sum(
        prob_rows.astype(jnp.float32) * own_select[:, None, None, :].astype(jnp.float32), axis=3
    ).reshape(MAXE, row_total)
    gate_spread, up_spread, down_spread = (
        lax.all_to_all(
            w_gate[0].reshape(width_share, group_total, piece_size),
            "group",
            split_axis=1,
            concat_axis=1,
            tiled=True,
        ),
        lax.all_to_all(
            w_up[0].reshape(width_share, group_total, piece_size),
            "group",
            split_axis=1,
            concat_axis=1,
            tiled=True,
        ),
        lax.all_to_all(
            w_down.reshape(1, group_total, piece_size * width_share),
            "group",
            split_axis=1,
            concat_axis=1,
            tiled=True,
        ),
    )
    slot_order = need_slot.T
    gate_sent = jnp.take(gate_spread, slot_order, axis=1)
    up_sent = jnp.take(up_spread, slot_order, axis=1)
    down_sent = jnp.take(down_spread, slot_order, axis=1)
    gate_got, up_got, down_got = (
        lax.all_to_all(gate_sent, "group", split_axis=2, concat_axis=2, tiled=True),
        lax.all_to_all(up_sent, "group", split_axis=2, concat_axis=2, tiled=True),
        lax.all_to_all(down_sent, "group", split_axis=2, concat_axis=2, tiled=True),
    )
    outcome, rows_dx, weight_gate, weight_up, weight_down = expert_pass(
        input_rows,
        rows_dy,
        rows_p,
        gate_got.reshape(width_share, MAXE, hidden_total),
        up_got.reshape(width_share, MAXE, hidden_total),
        down_got.reshape(MAXE, hidden_total, width_share),
    )
    back_gate, back_up, back_down = (
        lax.all_to_all(
            weight_gate.reshape(width_share, MAXE, group_total, piece_size),
            "group",
            split_axis=2,
            concat_axis=2,
            tiled=True,
        ),
        lax.all_to_all(
            weight_up.reshape(width_share, MAXE, group_total, piece_size),
            "group",
            split_axis=2,
            concat_axis=2,
            tiled=True,
        ),
        lax.all_to_all(
            weight_down.reshape(1, MAXE, group_total, piece_size * width_share),
            "group",
            split_axis=2,
            concat_axis=2,
            tiled=True,
        ),
    )
    slot_match = (
        (slot_order[:, :, None] == group_ids[None, None, :]) & (need_valid.T[:, :, None] > 0)
    ).astype(jnp.bfloat16)
    summed_gate = jnp.einsum(
        "dmgk,mgs->dsk", back_gate, slot_match, preferred_element_type=jnp.float32
    ).astype(jnp.bfloat16)
    summed_up = jnp.einsum(
        "dmgk,mgs->dsk", back_up, slot_match, preferred_element_type=jnp.float32
    ).astype(jnp.bfloat16)
    summed_down = jnp.einsum(
        "amgq,mgs->asq", back_down, slot_match, preferred_element_type=jnp.float32
    ).astype(jnp.bfloat16)
    home_gate, home_up, home_down = (
        lax.all_to_all(summed_gate, "group", split_axis=1, concat_axis=1, tiled=True),
        lax.all_to_all(summed_up, "group", split_axis=1, concat_axis=1, tiled=True),
        lax.all_to_all(summed_down, "group", split_axis=1, concat_axis=1, tiled=True),
    )
    grad_w_gate = home_gate.reshape(1, width_share, hidden_total)
    grad_w_up = home_up.reshape(1, width_share, hidden_total)
    grad_w_down = home_down.reshape(1, hidden_total, width_share)
    out_blocks = place_rows(
        outcome.reshape(MAXE, entry_total, BLK, width_share), listed, keep_rows, block_total
    )
    dx_blocks = place_rows(
        rows_dx.reshape(MAXE, entry_total, BLK, width_share), listed, keep_rows, block_total
    )
    layer_output = out_blocks.reshape(block_total * BLK, width_share).astype(jnp.bfloat16)
    grad_input = dx_blocks.reshape(block_total * BLK, width_share).astype(jnp.bfloat16)
    return (layer_output, grad_input, grad_w_gate, grad_w_up, grad_w_down)


def solution(mesh):
    in_specs = (
        P("group", "member"),
        P("group", "member"),
        P("group", None),
        P("group", "member", None),
        P("group", "member", None),
        P("group", None, "member"),
        P(),
        P(),
        P("group", None, None),
    )
    out_specs = (
        P("group", "member"),
        P("group", "member"),
        P("group", "member", None),
        P("group", "member", None),
        P("group", None, "member"),
    )
    return jax.shard_map(body, mesh=mesh, in_specs=in_specs, out_specs=out_specs, check_vma=False)
```

profile of v0, /device:TPU:1, one launch (start us, length us, event | category | flops | bytes accessed | tf_op | source)
XLA Modules:
  0.0 531.6 jit_solution(10994055985351064944)
XLA Ops:
  7.2 1.2 copy.255
  8.4 1.2 reshape.285
  10.1 3.4 reduce.2
  13.6 1.1 reshape.287
  14.7 12.0 %all-to-all-start.4 = ((bf16[16,2,7168]{2,1,0:T(2,128)(2,1)}), bf16[16,2,7168]{2,1,0:T(2,128)(2,1)S(1)}, u32[]{:S(2)}, u32[]{:S(2)}) async-start(bf16[16,2,7168]{2,1,0:T(2,128)(2,1)} %reshape.287), calls=%async_computation.4 | async-start | bytes 917504 | tf_op jit(solution)/shard_map/all_to_all | solution.py:115
  26.6 1.0 copy.244
  27.8 14.8 %all-to-all-done.4 = bf16[16,2,7168]{2,1,0:T(2,128)(2,1)S(1)} async-done(((bf16[16,2,7168]{2,1,0:T(2,128)(2,1)}), bf16[16,2,7168]{2,1,0:T(2,128)(2,1)S(1)}, u32[]{:S(2)}, u32[]{:S(2)}) %all-to-all-start.4) | async-done | bytes 458784 | tf_op jit(solution)/shard_map/all_to_all | solution.py:115
  42.6 3.5 all-to-all-start
  46.9 1.0 copy.250
  48.6 1.1 gather_fusion.1
  49.7 13.0 %all-to-all-done = bf16[224,16,64]{0,2,1:T(8,128)(2,1)S(1)} async-done(((bf16[224,16,64]{0,2,1:T(8,128)(2,1)}), bf16[224,16,64]{0,2,1:T(8,128)(2,1)S(1)}, u32[]{:S(2)}, u32[]{:S(2)}) %all-to-all-start) | async-done | bytes 458784 | tf_op jit(solution)/shard_map/all_to_all | solution.py:101
  62.7 3.5 all-to-all-start.2
  66.2 2.5 broadcast_select_fusion
  68.7 14.2 %all-to-all-done.2 = bf16[224,16,64]{0,2,1:T(8,128)(2,1)S(1)} async-done(((bf16[224,16,64]{0,2,1:T(8,128)(2,1)}), bf16[224,16,64]{0,2,1:T(8,128)(2,1)S(1)}, u32[]{:S(2)}, u32[]{:S(2)}) %all-to-all-start.2) | async-done | bytes 458784 | tf_op jit(solution)/shard_map/all_to_all | solution.py:108
  82.9 4.2 all-to-all-start.5
  88.7 1.1 copy.252
  89.8 21.5 %all-to-all-done.5 = bf16[1,2,16,14336]{3,1,0,2:T(2,128)(2,1)} async-done(((bf16[1,2,16,14336]{3,1,0,2:T(2,128)(2,1)}), bf16[1,2,16,14336]{3,1,0,2:T(2,128)(2,1)}, u32[]{:S(2)}, u32[]{:S(2)}) %all-to-all-start.5) | async-done | bytes 917536 | tf_op jit(solution)/shard_map/all_to_all | solution.py:130
  111.3 3.6 all-to-all-start.3
  115.5 1.0 copy.246
  116.5 26.2 %all-to-all-done.3 = bf16[224,2,16,64]{0,3,1,2:T(8,128)(2,1)S(1)} async-done(((bf16[224,2,16,64]{0,3,1,2:T(8,128)(2,1)}), bf16[224,2,16,64]{0,3,1,2:T(8,128)(2,1)S(1)}, u32[]{:S(2)}, u32[]{:S(2)}) %all-to-all-start.3) | async-done | bytes 917536 | tf_op jit(solution)/shard_map/all_to_all | solution.py:129
  142.7 3.6 all-to-all-start.1
  149.9 2.4 copy.259
  152.3 3.4 reshape.188
  156.8 1.6 convolution_convert_fusion.1
  158.4 15.8 %all-to-all-done.1 = bf16[224,2,16,64]{0,3,1,2:T(8,128)(2,1)S(1)} async-done(((bf16[224,2,16,64]{0,3,1,2:T(8,128)(2,1)}), bf16[224,2,16,64]{0,3,1,2:T(8,128)(2,1)S(1)}, u32[]{:S(2)}, u32[]{:S(2)}) %all-to-all-start.1) | async-done | bytes 917536 | tf_op jit(solution)/shard_map/all_to_all | solution.py:128
  174.3 1.7 convolution_convert_fusion.2
  176.2 1.6 convolution_convert_fusion
  177.8 167.9 %all-reduce.3.cloned.1.call-done = (bf16[2,320,1024]{2,1,0:T(8,128)(2,1)}, bf16[2,320,1024]{2,1,0:T(8,128)(2,1)}, bf16[2,320,1024]{2,1,0:T(8,128)(2,1)}) async-done(((bf16[2,320,1024]{2,1,0:T(8,128)(2,1)}, bf16[2,320,1024]{2,1,0:T(8,128)(2,1)}, bf16[2,320,1024]{2,1,0:T(8,128)(2,1)}), (bf16[2,320,1024]{2,1,0:T(8,128)(2,1)}, bf16[2,320,1024]{2,1,0:T(8,128)(2,1)}, ...) | async-done | bytes 3932176 | tf_op jit(solution)/shard_map/psum | solution.py:21
  345.7 5.0 fusion.11
  350.7 1.6 fusion.12
  352.3 2.2 copy.273
  354.5 3.3 copy.274
  357.8 10.6 %all-to-all-start.6 = ((bf16[224,2,16,64]{0,1,3,2:T(2,128)(2,1)}), bf16[224,2,16,64]{0,1,3,2:T(2,128)(2,1)}, u32[]{:S(2)}, u32[]{:S(2)}) async-start(bf16[224,2,16,64]{0,1,3,2:T(2,128)(2,1)} %copy.274), calls=%async_computation.6 | async-start | bytes 2097152 | tf_op jit(solution)/shard_map/all_to_all | solution.py:141
  368.5 1.6 fusion.13
  370.1 2.3 copy.277
  372.3 3.3 copy.278
  375.6 20.9 %all-to-all-done.6 = bf16[224,2,16,64]{0,1,3,2:T(2,128)(2,1)} async-done(((bf16[224,2,16,64]{0,1,3,2:T(2,128)(2,1)}), bf16[224,2,16,64]{0,1,3,2:T(2,128)(2,1)}, u32[]{:S(2)}, u32[]{:S(2)}) %all-to-all-start.6) | async-done | bytes 917536 | tf_op jit(solution)/shard_map/all_to_all | solution.py:141
  396.5 4.4 all-to-all-start.8
  400.9 2.9 convolution_convert_fusion.3
  403.9 2.3 copy.281
  406.1 3.4 reshape.196
  409.5 3.1 copy.282
  412.6 15.6 %all-to-all-done.8 = bf16[224,2,16,64]{0,1,3,2:T(2,128)(2,1)} async-done(((bf16[224,2,16,64]{0,1,3,2:T(2,128)(2,1)}), bf16[224,2,16,64]{0,1,3,2:T(2,128)(2,1)}, u32[]{:S(2)}, u32[]{:S(2)}) %all-to-all-start.8) | async-done | bytes 917536 | tf_op jit(solution)/shard_map/all_to_all | solution.py:148
  428.2 4.2 all-to-all-start.10
  432.6 1.9 fusion.17
  435.5 21.7 %all-to-all-done.10 = bf16[1,2,16,14336]{3,1,0,2:T(2,128)(2,1)} async-done(((bf16[1,2,16,14336]{3,1,0,2:T(2,128)(2,1)}), bf16[1,2,16,14336]{3,1,0,2:T(2,128)(2,1)}, u32[]{:S(2)}, u32[]{:S(2)}) %all-to-all-start.10) | async-done | bytes 917536 | tf_op jit(solution)/shard_map/all_to_all | solution.py:155
  457.2 3.5 all-to-all-start.7
  460.6 1.9 fusion.16
  462.5 1.0 copy.280
  463.5 14.3 %all-to-all-done.7 = bf16[224,16,64]{0,2,1:T(8,128)(2,1)S(1)} async-done(((bf16[224,16,64]{0,2,1:T(8,128)(2,1)}), bf16[224,16,64]{0,2,1:T(8,128)(2,1)S(1)}, u32[]{:S(2)}, u32[]{:S(2)}) %all-to-all-start.7) | async-done | bytes 458784 | tf_op jit(solution)/shard_map/all_to_all | solution.py:176
  477.8 4.1 all-to-all-start.9
  482.0 2.6 fusion.52
  484.5 1.6 fusion.1
  486.8 4.2 reduce.3
  491.0 2.1 reshape.289
  493.2 5.0 all-to-all-done.9
  498.2 4.3 all-to-all-start.11
  502.5 1.7 fusion.19
  507.3 1.0 copy.287
  508.2 2.0 copy.288
  510.2 7.1 %all-to-all-done.11 = bf16[16,2,7168]{2,1,0:T(2,128)(2,1)} async-done(((bf16[16,2,7168]{2,1,0:T(2,128)(2,1)}), bf16[16,2,7168]{2,1,0:T(2,128)(2,1)}, u32[]{:S(2)}, u32[]{:S(2)}) %all-to-all-start.11) | async-done | bytes 458784 | tf_op jit(solution)/shard_map/all_to_all | solution.py:178
  517.3 2.9 reshape.290
  520.2 2.6 bitcast_reduce_fusion
  523.6 1.0 copy.289
  (92 shorter events, 14.9 us)
Async XLA Ops:
  10.1 16.5 %copy-start.8 = (bf16[1,224,1024]{2,1,0:T(8,128)(2,1)S(1)}, bf16[1,224,1024]{2,1,0:T(8,128)(2,1)}, u32[]{:S(2)}) copy-start(bf16[1,224,1024]{2,1,0:T(8,128)(2,1)} %param.16) | copy-start | bytes 1376260
  13.5 14.1 %copy-start.13 = (s32[16,16]{1,0:T(8,128)S(1)}, s32[16,16]{1,0:T(8,128)}, u32[]{:S(2)}) copy-start(s32[16,16]{1,0:T(8,128)} %param.20) | copy-start | bytes 3076
  14.7 31.4 %copy-start.15 = (s32[16]{0:T(128)S(1)}, s32[16]{0:T(128)}, u32[]{:S(2)}) copy-start(s32[16]{0:T(128)} %param.19) | copy-start | bytes 196
  14.7 32.2 %copy-start.9 = (bf16[1,224,1024]{2,1,0:T(8,128)(2,1)S(1)}, bf16[1,224,1024]{2,1,0:T(8,128)(2,1)}, u32[]{:S(2)}) copy-start(bf16[1,224,1024]{2,1,0:T(8,128)(2,1)} %param.17) | copy-start | bytes 1376260
  14.7 27.9 %all-to-all-start.4 = ((bf16[16,2,7168]{2,1,0:T(2,128)(2,1)}), bf16[16,2,7168]{2,1,0:T(2,128)(2,1)S(1)}, u32[]{:S(2)}, u32[]{:S(2)}) async-start(bf16[16,2,7168]{2,1,0:T(2,128)(2,1)} %reshape.287), calls=%async_computation.4 | async-start | bytes 917504 | tf_op jit(solution)/shard_map/all_to_all | solution.py:115
  42.6 20.1 %all-to-all-start = ((bf16[224,16,64]{0,2,1:T(8,128)(2,1)}), bf16[224,16,64]{0,2,1:T(8,128)(2,1)S(1)}, u32[]{:S(2)}, u32[]{:S(2)}) async-start(bf16[224,16,64]{0,2,1:T(8,128)(2,1)} %bitcast.9), calls=%async_computation | async-start | bytes 1048576 | tf_op jit(solution)/shard_map/all_to_all | solution.py:101
  62.7 20.2 %all-to-all-start.2 = ((bf16[224,16,64]{0,2,1:T(8,128)(2,1)}), bf16[224,16,64]{0,2,1:T(8,128)(2,1)S(1)}, u32[]{:S(2)}, u32[]{:S(2)}) async-start(bf16[224,16,64]{0,2,1:T(8,128)(2,1)} %bitcast.13), calls=%async_computation.2 | async-start | bytes 1048576 | tf_op jit(solution)/shard_map/all_to_all | solution.py:108
  82.9 28.4 %all-to-all-start.5 = ((bf16[1,2,16,14336]{3,1,0,2:T(2,128)(2,1)}), bf16[1,2,16,14336]{3,1,0,2:T(2,128)(2,1)}, u32[]{:S(2)}, u32[]{:S(2)}) async-start(bf16[1,2,16,14336]{3,1,0,2:T(2,128)(2,1)} %broadcast_select_fusion), calls=%async_computation.5 | async-start | bytes 1835008 | tf_op jit(solution)/shard_map/all_to_all | solution.py:130
  89.8 25.1 %copy-start.14 = (s32[1,16,10]{1,0,2:T(1,128)S(1)}, s32[1,16,10]{1,0,2:T(1,128)}, u32[]{:S(2)}) copy-start(s32[1,16,10]{1,0,2:T(1,128)} %param.21) | copy-start | bytes 1924
  111.3 31.4 %all-to-all-start.3 = ((bf16[224,2,16,64]{0,3,1,2:T(8,128)(2,1)}), bf16[224,2,16,64]{0,3,1,2:T(8,128)(2,1)S(1)}, u32[]{:S(2)}, u32[]{:S(2)}) async-start(bf16[224,2,16,64]{0,3,1,2:T(8,128)(2,1)} %copy.252), calls=%async_computation.3 | async-start | bytes 2097152 | tf_op jit(solution)/shard_map/all_to_all | solution.py:129
  116.5 30.5 %copy-start.12 = (bf16[512,16]{0,1:T(8,128)(2,1)S(1)}, bf16[512,16]{0,1:T(8,128)(2,1)}, u32[]{:S(2)}) copy-start(bf16[512,16]{0,1:T(8,128)(2,1)} %param.15) | copy-start | bytes 49156
  116.5 31.6 %copy-start.10 = (bf16[512,224]{0,1:T(8,128)(2,1)S(1)}, bf16[512,224]{0,1:T(8,128)(2,1)}, u32[]{:S(2)}) copy-start(bf16[512,224]{0,1:T(8,128)(2,1)} %param.13) | copy-start | bytes 688132
  116.5 31.8 %copy-start.11 = (bf16[512,224]{0,1:T(8,128)(2,1)S(1)}, bf16[512,224]{0,1:T(8,128)(2,1)}, u32[]{:S(2)}) copy-start(bf16[512,224]{0,1:T(8,128)(2,1)} %param.14) | copy-start | bytes 688132
  142.7 31.5 %all-to-all-start.1 = ((bf16[224,2,16,64]{0,3,1,2:T(8,128)(2,1)}), bf16[224,2,16,64]{0,3,1,2:T(8,128)(2,1)S(1)}, u32[]{:S(2)}, u32[]{:S(2)}) async-start(bf16[224,2,16,64]{0,3,1,2:T(8,128)(2,1)} %copy.246), calls=%async_computation.1 | async-start | bytes 2097152 | tf_op jit(solution)/shard_map/all_to_all | solution.py:128
  146.3 199.4 %all-reduce.3.cloned.1.call-start = ((), (), s32[]{:S(2)}) async-start(), calls=%async_computation.12 | async-start | bytes 7864320 | tf_op jit(solution)/shard_map/psum | solution.py:21
  155.8 1.0 copy-start
  174.3 1.7 copy-start.2
  174.3 1.9 copy-start.4
  357.8 38.7 %all-to-all-start.6 = ((bf16[224,2,16,64]{0,1,3,2:T(2,128)(2,1)}), bf16[224,2,16,64]{0,1,3,2:T(2,128)(2,1)}, u32[]{:S(2)}, u32[]{:S(2)}) async-start(bf16[224,2,16,64]{0,1,3,2:T(2,128)(2,1)} %copy.274), calls=%async_computation.6 | async-start | bytes 2097152 | tf_op jit(solution)/shard_map/all_to_all | solution.py:141
  396.5 31.7 %all-to-all-start.8 = ((bf16[224,2,16,64]{0,1,3,2:T(2,128)(2,1)}), bf16[224,2,16,64]{0,1,3,2:T(2,128)(2,1)}, u32[]{:S(2)}, u32[]{:S(2)}) async-start(bf16[224,2,16,64]{0,1,3,2:T(2,128)(2,1)} %copy.278), calls=%async_computation.8 | async-start | bytes 2097152 | tf_op jit(solution)/shard_map/all_to_all | solution.py:148
  428.2 28.9 %all-to-all-start.10 = ((bf16[1,2,16,14336]{3,1,0,2:T(2,128)(2,1)}), bf16[1,2,16,14336]{3,1,0,2:T(2,128)(2,1)}, u32[]{:S(2)}, u32[]{:S(2)}) async-start(bf16[1,2,16,14336]{3,1,0,2:T(2,128)(2,1)} %copy.282), calls=%async_computation.10 | async-start | bytes 1835008 | tf_op jit(solution)/shard_map/all_to_all | solution.py:155
  457.2 20.7 %all-to-all-start.7 = ((bf16[224,16,64]{0,2,1:T(8,128)(2,1)}), bf16[224,16,64]{0,2,1:T(8,128)(2,1)S(1)}, u32[]{:S(2)}, u32[]{:S(2)}) async-start(bf16[224,16,64]{0,2,1:T(8,128)(2,1)} %copy.276), calls=%async_computation.7 | async-start | bytes 1048576 | tf_op jit(solution)/shard_map/all_to_all | solution.py:176
  477.8 6.7 %copy-start.6 = (bf16[224,16,64]{0,2,1:T(8,128)(2,1)}, bf16[224,16,64]{0,2,1:T(8,128)(2,1)S(1)}, u32[]{:S(2)}) copy-start(bf16[224,16,64]{0,2,1:T(8,128)(2,1)S(1)} %all-to-all-done.7) | copy-start | bytes 1376260
  477.8 20.3 %all-to-all-start.9 = ((bf16[224,16,64]{0,2,1:T(8,128)(2,1)}), bf16[224,16,64]{0,2,1:T(8,128)(2,1)}, u32[]{:S(2)}, u32[]{:S(2)}) async-start(bf16[224,16,64]{0,2,1:T(8,128)(2,1)} %copy.280), calls=%async_computation.9 | async-start | bytes 1048576 | tf_op jit(solution)/shard_map/all_to_all | solution.py:177
  486.8 15.7 %copy-start.1 = (bf16[224,2,16,64]{0,3,2,1:T(8,128)(2,1)S(1)}, bf16[224,2,16,64]{0,3,2,1:T(8,128)(2,1)}, u32[]{:S(2)}) copy-start(bf16[224,2,16,64]{0,3,2,1:T(8,128)(2,1)} %copy-done) | copy-start | bytes 2752516
  498.2 19.2 %all-to-all-start.11 = ((bf16[16,2,7168]{2,1,0:T(2,128)(2,1)}), bf16[16,2,7168]{2,1,0:T(2,128)(2,1)}, u32[]{:S(2)}, u32[]{:S(2)}) async-start(bf16[16,2,7168]{2,1,0:T(2,128)(2,1)} %reshape.289), calls=%async_computation.11 | async-start | bytes 917504 | tf_op jit(solution)/shard_map/all_to_all | solution.py:178
  502.5 2.9 copy-start.5
  504.2 1.3 copy-start.3
  506.0 1.2 copy-start.7
Sparse Core Ops, SparseCore 0:
  177.9 167.7 all-reduce.2
where the time goes:
time: 540 us; the launch traced here: 532 us
  waiting for transfers between devices  358 us (66%)
  starting transfers between devices  61.9 us (11%)
  local copies, waits for them, and re-layouts  58.1 us (11%)
  matrix products  21.8 us (4%)
  other arithmetic  17.1 us (3%)
  between operations  14.8 us (3%)
    psum x1, waiting for transfers between devices, expert_pass(): lax.psum(part_up.astype(jnp.bfloat16), 'member').astype(jnp.float32)  168 us
    all_to_all x1, waiting for transfers between devices, body(): lax.all_to_all(up_sent, 'group', split_axis=2, concat_axis=2, tiled=True)  26.2 us
    all_to_all x1, waiting for transfers between devices, body(): lax.all_to_all(weight_down.reshape(1, MAXE, group_total, piece_size * wid...  21.7 us
    all_to_all x1, waiting for transfers between devices, body(): lax.all_to_all(down_sent, 'group', split_axis=2, concat_axis=2, tiled=True)  21.5 us
    all_to_all x1, waiting for transfers between devices, body(): lax.all_to_all(weight_gate.reshape(width_share, MAXE, group_total, piece_...  20.9 us
    unnamed x49, local copies, waits for them, and re-layouts  17.7 us
    all_to_all x1, waiting for transfers between devices, body(): lax.all_to_all(gate_sent, 'group', split_axis=2, concat_axis=2, tiled=True)  15.8 us
    all_to_all x1, waiting for transfers between devices, body(): lax.all_to_all(weight_up.reshape(width_share, MAXE, group_total, piece_si...  15.6 us
  transfers between devices with their start and end apart: 13, of which 13 were waited for; matrix products, arithmetic and copies ran while one was open for 12% of the time, Pallas kernels for 0%

commit v1 on v0

--- a/solution.py
+++ b/solution.py
@@ -18,7 +18,7 @@
     part_up = jnp.einsum(form_in, input_rows, up_w, preferred_element_type=jnp.float32)
     gate, up = (
         lax.psum(part_gate.astype(jnp.bfloat16), "member").astype(jnp.float32),
-        lax.psum(part_up.astype(jnp.bfloat16), "member").astype(jnp.float32),
+        jnp.sum(lax.all_gather(part_up.astype(jnp.bfloat16), "member"), axis=0).astype(jnp.float32),
     )
     sigma = jax.nn.sigmoid(gate)
     hidden_state = (gate * sigma * up).astype(jnp.bfloat16)

time: 540 us -> 741 us (1.37)
  waiting for transfers between devices: 358 us -> 527 us
  blocking collectives: 0 us -> 19.3 us
  other arithmetic: 17.1 us -> 34.8 us
    all_gather x0 -> x1, waiting for transfers between devices: none -> 192 us  [expert_pass(): lax.all_gather(part_up.astype(jnp.bfloat16), 'member')]
    all_to_all x0 -> x1, blocking collectives: none -> 19.3 us  [body(): lax.all_to_all(w_down.reshape(1, group_total, piece_size * width_share),...]
    psum x1, waiting for transfers between devices: 168 us -> 150 us  [expert_pass(): lax.psum(part_gate.astype(jnp.bfloat16), 'member').astype(jnp.float32)]
    reduce_sum x0 -> x1, other arithmetic: none -> 15 us  [expert_pass(): jnp.sum(lax.all_gather(part_up.astype(jnp.bfloat16), 'member'), axis=0)]
    all_to_all x1 -> x0, waiting for transfers between devices: 14.8 us -> none  [body(): lax.all_to_all(w_down.reshape(1, group_total, piece_size * width_share),...]
    all_to_all x1 -> x0, starting transfers between devices: 12 us -> none  [body(): lax.all_to_all(w_down.reshape(1, group_total, piece_size * width_share),...]
    all_to_all x1, starting transfers between devices: 3.47 us -> 12 us  [body(): lax.all_to_all(w_gate[0].reshape(width_share, group_total, piece_size), '...]
    all_to_all x1, waiting for transfers between devices: 15.8 us -> 23.5 us  [body(): lax.all_to_all(gate_sent, 'group', split_axis=2, concat_axis=2, tiled=True)]
  transfers between devices with their start and end apart: 13 -> 13, of which waited for: 13 -> 13; matrix products, arithmetic and copies ran while one was open for 12% -> 11% of each run, Pallas kernels for 0% -> 0%
where the time goes in v1:
time: 741 us; the launch traced here: 732 us
  waiting for transfers between devices  527 us (71%)
  starting transfers between devices  59.2 us (8%)
  local copies, waits for them, and re-layouts  55 us (7%)
  other arithmetic  34.8 us (5%)
  matrix products  21.8 us (3%)
  blocking collectives  19.3 us (3%)
  between operations  14.8 us (2%)
    all_gather x1, waiting for transfers between devices, expert_pass(): lax.all_gather(part_up.astype(jnp.bfloat16), 'member')  192 us
    psum x1, waiting for transfers between devices, expert_pass(): lax.psum(part_gate.astype(jnp.bfloat16), 'member').astype(jnp.float32)  150 us
    all_to_all x1, waiting for transfers between devices, body(): lax.all_to_all(up_sent, 'group', split_axis=2, concat_axis=2, tiled=True)  24.7 us
    all_to_all x1, waiting for transfers between devices, body(): lax.all_to_all(down_sent, 'group', split_axis=2, concat_axis=2, tiled=True)  23.5 us
    all_to_all x1, waiting for transfers between devices, body(): lax.all_to_all(gate_sent, 'group', split_axis=2, concat_axis=2, tiled=True)  23.5 us
    all_to_all x1, waiting for transfers between devices, body(): lax.all_to_all(weight_down.reshape(1, MAXE, group_total, piece_size * wid...  21.6 us
    all_to_all x1, waiting for transfers between devices, body(): lax.all_to_all(weight_gate.reshape(width_share, MAXE, group_total, piece_...  20.9 us
    all_to_all x1, blocking collectives, body(): lax.all_to_all(w_down.reshape(1, group_total, piece_size * width_share),...  19.3 us
  transfers between devices with their start and end apart: 13, of which 13 were waited for; matrix products, arithmetic and copies ran while one was open for 11% of the time, Pallas kernels for 0%

profile of v1, /device:TPU:1, one launch (start us, length us, event | category | flops | bytes accessed | tf_op | source)
XLA Modules:
  0.0 731.9 jit_solution(9866844518494905146)
XLA Ops:
  7.2 2.1 copy.244
  9.3 12.0 %all-to-all-start = ((bf16[224,16,64]{0,2,1:T(8,128)(2,1)}), bf16[224,16,64]{0,2,1:T(8,128)(2,1)S(1)}, u32[]{:S(2)}, u32[]{:S(2)}) async-start(bf16[224,16,64]{0,2,1:T(8,128)(2,1)} %bitcast.9), calls=%async_computation | async-start | bytes 1048576 | tf_op jit(solution)/shard_map/all_to_all | solution.py:101
  21.2 1.0 copy.250
  22.4 16.1 %all-to-all-done = bf16[224,16,64]{0,2,1:T(8,128)(2,1)S(1)} async-done(((bf16[224,16,64]{0,2,1:T(8,128)(2,1)}), bf16[224,16,64]{0,2,1:T(8,128)(2,1)S(1)}, u32[]{:S(2)}, u32[]{:S(2)}) %all-to-all-start) | async-done | bytes 458784 | tf_op jit(solution)/shard_map/all_to_all | solution.py:101
  38.6 3.5 all-to-all-start.2
  43.6 15.1 %all-to-all-done.2 = bf16[224,16,64]{0,2,1:T(8,128)(2,1)S(1)} async-done(((bf16[224,16,64]{0,2,1:T(8,128)(2,1)}), bf16[224,16,64]{0,2,1:T(8,128)(2,1)S(1)}, u32[]{:S(2)}, u32[]{:S(2)}) %all-to-all-start.2) | async-done | bytes 458784 | tf_op jit(solution)/shard_map/all_to_all | solution.py:108
  59.4 1.2 select_bitcast_fusion.1
  60.6 1.1 copy.252
  61.7 3.7 all-to-all-start.3
  67.9 24.7 %all-to-all-done.3 = bf16[224,2,16,64]{0,3,1,2:T(8,128)(2,1)S(1)} async-done(((bf16[224,2,16,64]{0,3,1,2:T(8,128)(2,1)}), bf16[224,2,16,64]{0,3,1,2:T(8,128)(2,1)S(1)}, u32[]{:S(2)}, u32[]{:S(2)}) %all-to-all-start.3) | async-done | bytes 917536 | tf_op jit(solution)/shard_map/all_to_all | solution.py:129
  93.7 1.6 convolution_convert_fusion.1
  95.4 1.0 copy-done.11
  96.6 1.2 reshape.286
  98.3 3.4 reduce.3
  102.0 19.3 %all_to_all.60 = bf16[16,2,7168]{2,1,0:T(2,128)(2,1)S(1)} all-to-all(bf16[16,2,7168]{2,1,0:T(2,128)(2,1)S(1)} %reshape.288), channel_id=1, replica_groups=mesh['group'=16,'member'=32] {'group'}, dimensions={0} | all-to-all | bytes 917504 | tf_op jit(solution)/shard_map/all_to_all | solution.py:115
  122.0 1.1 gather_fusion.1
  123.1 2.5 broadcast_select_fusion
  125.6 3.7 all-to-all-start.5
  129.3 1.1 copy.246
  130.3 23.5 %all-to-all-done.5 = bf16[1,2,16,14336]{3,1,0,2:T(2,128)(2,1)S(1)} async-done(((bf16[1,2,16,14336]{3,1,0,2:T(2,128)(2,1)}), bf16[1,2,16,14336]{3,1,0,2:T(2,128)(2,1)S(1)}, u32[]{:S(2)}, u32[]{:S(2)}) %all-to-all-start.5) | async-done | bytes 917536 | tf_op jit(solution)/shard_map/all_to_all | solution.py:130
  153.9 3.6 all-to-all-start.1
  160.1 1.5 reshape.188
  161.6 23.5 %all-to-all-done.1 = bf16[224,2,16,64]{0,3,1,2:T(8,128)(2,1)S(1)} async-done(((bf16[224,2,16,64]{0,3,1,2:T(8,128)(2,1)}), bf16[224,2,16,64]{0,3,1,2:T(8,128)(2,1)S(1)}, u32[]{:S(2)}, u32[]{:S(2)}) %all-to-all-start.1) | async-done | bytes 917536 | tf_op jit(solution)/shard_map/all_to_all | solution.py:128
  185.3 1.6 convolution_convert_fusion.2
  186.9 1.6 convolution_convert_fusion
  188.6 191.6 %all-gather.3.cloned.1.call-done = bf16[64,320,1024]{2,1,0:T(8,128)(2,1)} async-done(((bf16[2,320,1024]{2,1,0:T(8,128)(2,1)}), bf16[64,320,1024]{2,1,0:T(8,128)(2,1)}) %all-gather.3.cloned.1.call-update) | async-done | bytes 41943056 | tf_op jit(solution)/shard_map/all_gather | solution.py:21
  380.2 15.0 %reduce_sum.64 = bf16[2,320,1024]{2,1,0:T(8,128)(2,1)} reduce(bf16[32,2,320,1024]{3,2,1,0:T(8,128)(2,1)} %bitcast.131, bf16[]{:T(256)} %constant.78.clone.1), dimensions={0}, to_apply=%region_6.9 | reduce | flops 20316160 | bytes 43253760 | tf_op jit(solution)/shard_map/reduce_sum | solution.py:21
  395.2 149.7 %all-reduce.3.cloned.1.call-done = (bf16[2,320,1024]{2,1,0:T(8,128)(2,1)}, bf16[2,320,1024]{2,1,0:T(8,128)(2,1)}) async-done(((bf16[2,320,1024]{2,1,0:T(8,128)(2,1)}, bf16[2,320,1024]{2,1,0:T(8,128)(2,1)}), (bf16[2,320,1024]{2,1,0:T(8,128)(2,1)}, bf16[2,320,1024]{2,1,0:T(8,128)(2,1)})) %all-reduce.3.cloned.1.call-update) | async-done | bytes 2621456 | tf_op jit(solution)/shard_map/psum | solution.py:20
  544.9 5.0 fusion.11
  549.8 1.6 fusion.12
  551.5 2.2 copy.273
  553.7 3.3 copy.274
  556.9 11.7 %all-to-all-start.6 = ((bf16[224,2,16,64]{0,1,3,2:T(2,128)(2,1)}), bf16[224,2,16,64]{0,1,3,2:T(2,128)(2,1)}, u32[]{:S(2)}, u32[]{:S(2)}) async-start(bf16[224,2,16,64]{0,1,3,2:T(2,128)(2,1)} %copy.274), calls=%async_computation.6 | async-start | bytes 2097152 | tf_op jit(solution)/shard_map/all_to_all | solution.py:141
  568.7 1.6 fusion.13
  570.3 2.3 copy.277
  572.6 3.3 copy.278
  575.9 20.9 %all-to-all-done.6 = bf16[224,2,16,64]{0,1,3,2:T(2,128)(2,1)} async-done(((bf16[224,2,16,64]{0,1,3,2:T(2,128)(2,1)}), bf16[224,2,16,64]{0,1,3,2:T(2,128)(2,1)}, u32[]{:S(2)}, u32[]{:S(2)}) %all-to-all-start.6) | async-done | bytes 917536 | tf_op jit(solution)/shard_map/all_to_all | solution.py:141
  596.7 4.4 all-to-all-start.8
  601.1 2.9 convolution_convert_fusion.3
  604.1 2.3 copy.281
  606.3 3.4 reshape.196
  609.7 3.1 copy.282
  612.8 15.7 %all-to-all-done.8 = bf16[224,2,16,64]{0,1,3,2:T(2,128)(2,1)} async-done(((bf16[224,2,16,64]{0,1,3,2:T(2,128)(2,1)}), bf16[224,2,16,64]{0,1,3,2:T(2,128)(2,1)}, u32[]{:S(2)}, u32[]{:S(2)}) %all-to-all-start.8) | async-done | bytes 917536 | tf_op jit(solution)/shard_map/all_to_all | solution.py:148
  628.4 4.2 all-to-all-start.10
  632.8 1.9 fusion.17
  634.7 1.0 copy.276
  635.7 21.6 %all-to-all-done.10 = bf16[1,2,16,14336]{3,1,0,2:T(2,128)(2,1)} async-done(((bf16[1,2,16,14336]{3,1,0,2:T(2,128)(2,1)}), bf16[1,2,16,14336]{3,1,0,2:T(2,128)(2,1)}, u32[]{:S(2)}, u32[]{:S(2)}) %all-to-all-start.10) | async-done | bytes 917536 | tf_op jit(solution)/shard_map/all_to_all | solution.py:155
  657.4 3.5 all-to-all-start.7
  660.8 1.9 fusion.16
  662.7 1.0 copy.280
  663.7 14.3 %all-to-all-done.7 = bf16[224,16,64]{0,2,1:T(8,128)(2,1)S(1)} async-done(((bf16[224,16,64]{0,2,1:T(8,128)(2,1)}), bf16[224,16,64]{0,2,1:T(8,128)(2,1)S(1)}, u32[]{:S(2)}, u32[]{:S(2)}) %all-to-all-start.7) | async-done | bytes 458784 | tf_op jit(solution)/shard_map/all_to_all | solution.py:176
  678.0 4.1 all-to-all-start.9
  682.2 2.6 fusion.52
  684.7 1.6 fusion.1
  686.3 1.7 copy.320
  688.0 5.3 reduce.4
  693.2 2.1 reshape.290
  695.4 3.0 all-to-all-done.9
  698.4 4.3 all-to-all-start.11
  704.6 1.7 fusion.18
  708.5 2.0 copy.288
  710.5 7.1 all-to-all-done.11
  717.6 2.9 reshape.291
  720.5 2.6 bitcast_reduce_fusion
  (99 shorter events, 16.2 us)
Async XLA Ops:
  7.2 14.1 %copy-start.10 = (bf16[1,224,1024]{2,1,0:T(8,128)(2,1)S(1)}, bf16[1,224,1024]{2,1,0:T(8,128)(2,1)}, u32[]{:S(2)}) copy-start(bf16[1,224,1024]{2,1,0:T(8,128)(2,1)} %param.17) | copy-start | bytes 1376260
  7.2 15.1 %copy-start.15 = (s32[16,16]{1,0:T(8,128)S(1)}, s32[16,16]{1,0:T(8,128)}, u32[]{:S(2)}) copy-start(s32[16,16]{1,0:T(8,128)} %param.20) | copy-start | bytes 3076
  9.3 32.8 %copy-start.17 = (s32[16]{0:T(128)S(1)}, s32[16]{0:T(128)}, u32[]{:S(2)}) copy-start(s32[16]{0:T(128)} %param.19) | copy-start | bytes 196
  9.3 29.3 %all-to-all-start = ((bf16[224,16,64]{0,2,1:T(8,128)(2,1)}), bf16[224,16,64]{0,2,1:T(8,128)(2,1)S(1)}, u32[]{:S(2)}, u32[]{:S(2)}) async-start(bf16[224,16,64]{0,2,1:T(8,128)(2,1)} %bitcast.9), calls=%async_computation | async-start | bytes 1048576 | tf_op jit(solution)/shard_map/all_to_all | solution.py:101
  38.6 20.2 %all-to-all-start.2 = ((bf16[224,16,64]{0,2,1:T(8,128)(2,1)}), bf16[224,16,64]{0,2,1:T(8,128)(2,1)S(1)}, u32[]{:S(2)}, u32[]{:S(2)}) async-start(bf16[224,16,64]{0,2,1:T(8,128)(2,1)} %bitcast.13), calls=%async_computation.2 | async-start | bytes 1048576 | tf_op jit(solution)/shard_map/all_to_all | solution.py:108
  61.7 3.8 copy-start.16
  61.7 4.4 copy-start.12
  61.7 4.6 copy-start.13
  61.7 31.0 %all-to-all-start.3 = ((bf16[224,2,16,64]{0,3,1,2:T(8,128)(2,1)}), bf16[224,2,16,64]{0,3,1,2:T(8,128)(2,1)S(1)}, u32[]{:S(2)}, u32[]{:S(2)}) async-start(bf16[224,2,16,64]{0,3,1,2:T(8,128)(2,1)} %copy.252), calls=%async_computation.3 | async-start | bytes 2097152 | tf_op jit(solution)/shard_map/all_to_all | solution.py:129
  65.4 314.8 %all-gather.3.cloned.1.call-start = ((), (), s32[]{:S(2)}) async-start(), calls=%async_computation.12 | async-start | bytes 43253760 | tf_op jit(solution)/shard_map/all_gather | solution.py:21
  92.8 1.0 copy-start
  95.4 1.0 copy-start.11
  125.6 3.7 copy-start.4
  125.6 28.3 %all-to-all-start.5 = ((bf16[1,2,16,14336]{3,1,0,2:T(2,128)(2,1)}), bf16[1,2,16,14336]{3,1,0,2:T(2,128)(2,1)S(1)}, u32[]{:S(2)}, u32[]{:S(2)}) async-start(bf16[1,2,16,14336]{3,1,0,2:T(2,128)(2,1)} %broadcast_select_fusion), calls=%async_computation.5 | async-start | bytes 1835008 | tf_op jit(solution)/shard_map/all_to_all | solution.py:130
  130.3 27.7 %copy-start.14 = (bf16[512,16]{0,1:T(8,128)(2,1)S(1)}, bf16[512,16]{0,1:T(8,128)(2,1)}, u32[]{:S(2)}) copy-start(bf16[512,16]{0,1:T(8,128)(2,1)} %param.15) | copy-start | bytes 49156
  153.9 31.3 %all-to-all-start.1 = ((bf16[224,2,16,64]{0,3,1,2:T(8,128)(2,1)}), bf16[224,2,16,64]{0,3,1,2:T(8,128)(2,1)S(1)}, u32[]{:S(2)}, u32[]{:S(2)}) async-start(bf16[224,2,16,64]{0,3,1,2:T(8,128)(2,1)} %copy.246), calls=%async_computation.1 | async-start | bytes 2097152 | tf_op jit(solution)/shard_map/all_to_all | solution.py:128
  157.4 387.5 %all-reduce.3.cloned.1.call-start = ((), (), s32[]{:S(2)}) async-start(), calls=%async_computation.13 | async-start | bytes 5242880 | tf_op jit(solution)/shard_map/psum | solution.py:20
  161.6 25.3 %copy-start.5 = (bf16[2,1024,224]{2,1,0:T(8,128)(2,1)}, bf16[2,1024,224]{2,1,0:T(8,128)(2,1)S(1)}, u32[]{:S(2)}) copy-start(bf16[2,1024,224]{2,1,0:T(8,128)(2,1)S(1)} %reshape.188) | copy-start | bytes 2752516
  185.3 1.7 copy-start.2
  185.3 1.7 copy-start.6
  556.9 39.8 %all-to-all-start.6 = ((bf16[224,2,16,64]{0,1,3,2:T(2,128)(2,1)}), bf16[224,2,16,64]{0,1,3,2:T(2,128)(2,1)}, u32[]{:S(2)}, u32[]{:S(2)}) async-start(bf16[224,2,16,64]{0,1,3,2:T(2,128)(2,1)} %copy.274), calls=%async_computation.6 | async-start | bytes 2097152 | tf_op jit(solution)/shard_map/all_to_all | solution.py:141
  596.7 31.7 %all-to-all-start.8 = ((bf16[224,2,16,64]{0,1,3,2:T(2,128)(2,1)}), bf16[224,2,16,64]{0,1,3,2:T(2,128)(2,1)}, u32[]{:S(2)}, u32[]{:S(2)}) async-start(bf16[224,2,16,64]{0,1,3,2:T(2,128)(2,1)} %copy.278), calls=%async_computation.8 | async-start | bytes 2097152 | tf_op jit(solution)/shard_map/all_to_all | solution.py:148
  628.4 28.9 %all-to-all-start.10 = ((bf16[1,2,16,14336]{3,1,0,2:T(2,128)(2,1)}), bf16[1,2,16,14336]{3,1,0,2:T(2,128)(2,1)}, u32[]{:S(2)}, u32[]{:S(2)}) async-start(bf16[1,2,16,14336]{3,1,0,2:T(2,128)(2,1)} %copy.282), calls=%async_computation.10 | async-start | bytes 1835008 | tf_op jit(solution)/shard_map/all_to_all | solution.py:155
  657.4 20.7 %all-to-all-start.7 = ((bf16[224,16,64]{0,2,1:T(8,128)(2,1)}), bf16[224,16,64]{0,2,1:T(8,128)(2,1)S(1)}, u32[]{:S(2)}, u32[]{:S(2)}) async-start(bf16[224,16,64]{0,2,1:T(8,128)(2,1)} %copy.276), calls=%async_computation.7 | async-start | bytes 1048576 | tf_op jit(solution)/shard_map/all_to_all | solution.py:176
  678.0 6.7 copy-start.8
  678.0 20.3 %all-to-all-start.9 = ((bf16[224,16,64]{0,2,1:T(8,128)(2,1)}), bf16[224,16,64]{0,2,1:T(8,128)(2,1)}, u32[]{:S(2)}, u32[]{:S(2)}) async-start(bf16[224,16,64]{0,2,1:T(8,128)(2,1)} %copy.280), calls=%async_computation.9 | async-start | bytes 1048576 | tf_op jit(solution)/shard_map/all_to_all | solution.py:177
  688.0 14.7 %copy-start.1 = (bf16[224,2,16,64]{0,3,2,1:T(8,128)(2,1)S(1)}, bf16[224,2,16,64]{0,3,2,1:T(8,128)(2,1)}, u32[]{:S(2)}) copy-start(bf16[224,2,16,64]{0,3,2,1:T(8,128)(2,1)} %copy-done) | copy-start | bytes 2752516
  688.0 14.7 %copy-start.7 = (f32[2,320,224]{2,1,0:T(8,128)S(1)}, f32[2,320,224]{2,1,0:T(8,128)}, u32[]{:S(2)}) copy-start(f32[2,320,224]{2,1,0:T(8,128)} %fusion.52) | copy-start | bytes 1720324
  698.4 19.3 %all-to-all-start.11 = ((bf16[16,2,7168]{2,1,0:T(2,128)(2,1)}), bf16[16,2,7168]{2,1,0:T(2,128)(2,1)}, u32[]{:S(2)}, u32[]{:S(2)}) async-start(bf16[16,2,7168]{2,1,0:T(2,128)(2,1)} %reshape.290), calls=%async_computation.11 | async-start | bytes 917504 | tf_op jit(solution)/shard_map/all_to_all | solution.py:178
  703.2 1.3 copy-start.3
  706.3 1.2 copy-start.9
Sparse Core Ops, SparseCore 0:
  95.5 284.6 all-gather.2
  383.9 160.9 all-reduce.2
